TPU v7x, 256 devices: a whole 4x4x8 slice. The times are simulated.
256 devices in a mesh: gx: 16 (over x, y), gy: 2 (over core), gz: 8 (over z).
Axes of the slice: x: 4, y: 4, z: 8, core: 2. Of those that a mesh axis runs over, the one named last changes fastest.
Arguments:
- field: float32 [2, 1024, 128, 1024], P(None, 'gx', 'gy', 'gz'), as said below
- start_basis: float32 [1024, 256], replicated, may hold values from -6 to 6
Outputs:
- factor: float32 [1024, 256], P('gx')
- core: float32 [2, 256, 128, 1024], P(None, 'gx', 'gy', 'gz')
Inputs may be any that keep to these rules, and one draw needn't show every extreme that they name: Real-valued field; no structure is promised.
All inputs are finite; a program needn't handle non-finite values.
Results may differ from a plain program's by a relative error of at most 0.0002.
Values sent between devices are 32-bit elements; how exact they have to be, the bound alone decides.
A program may use at most 64 MiB of HBM per device.

v0:
```python
import jax
import jax.numpy as jnp
from jax import lax
from jax.sharding import PartitionSpec as P

ITERS = 2


def orthonormal(image):
    small = jnp.dot(image.T, image, precision=lax.Precision.HIGHEST)
    lower = jnp.linalg.cholesky(small)
    return jax.scipy.linalg.solve_triangular(lower, image.T, lower=True).T


def per_device(field, start_basis):
    comps, slab, cells_y, cells_z = field.shape
    flat_field = field.reshape(comps, slab, cells_y * cells_z)
    fibers = lax.all_to_all(flat_field, "gx", split_axis=2, concat_axis=1, tiled=True)
    basis = start_basis
    local_gram = jnp.einsum("crm,csm->rs", fibers, fibers, precision=lax.Precision.HIGHEST)
    gram = lax.psum(local_gram, ("gx", "gy", "gz"))
    for step in range(ITERS):
        image = jnp.dot(gram, basis, precision=lax.Precision.HIGHEST)
        basis = orthonormal(image)
    projected = jnp.einsum("rk,crm->ckm", basis, fibers, precision=lax.Precision.HIGHEST)
    returned = lax.all_to_all(projected, "gx", split_axis=1, concat_axis=2, tiled=True)
    offset = lax.axis_index("gx") * slab
    factor = lax.dynamic_slice_in_dim(basis, offset, slab, 0)
    return (factor, returned.reshape(comps, returned.shape[1], cells_y, cells_z))


def solution(mesh):
    placed = (P(None, "gx", "gy", "gz"), P())
    return jax.shard_map(
        per_device,
        mesh=mesh,
        in_specs=placed,
        out_specs=(P("gx", None), P(None, "gx", "gy", "gz")),
        check_vma=False,
    )
```

profile of v0, /device:TPU:97, one launch (start us, length us, event | category | flops | bytes accessed | tf_op | source)
XLA Modules:
  0.0 604.0 jit_solution(12621777568615691695)
XLA Ops:
  7.2 0.0 copy-start
  7.2 0.0 all-reduce.3.cloned.1.call-start
  7.2 8.4 %copy.13 = f32[2,64,64,128]{1,0,3,2:T(2,128)} copy(f32[2,64,64,128]{3,2,1,0:T(8,128)} %param.5) | data formatting | bytes 8388608 | tf_op args[0]
  15.7 15.1 %reshape.52 = f32[16,1,65536]{2,1,0:T(1,128)} reshape(f32[8192,2,64]{2,1,0:T(2,128)} %bitcast.97) | data formatting | bytes 8388608
  30.8 56.1 %all_to_all.33 = f32[16,1,65536]{2,1,0:T(1,128)} all-to-all(f32[16,1,65536]{2,1,0:T(1,128)} %reshape.52), channel_id=1, replica_groups=mesh['gx'=16,'gy'=2,'gz'=8] {'gx'}, dimensions={0} | all-to-all | bytes 8388608 | tf_op jit(solution)/shard_map/all_to_all | solution.py:18
  86.8 0.5 broadcast.87
  87.3 13.7 %reduce.8 = f32[16,65536]{1,0:T(8,128)} reduce(f32[16,1,65536]{2,1,0:T(1,128)} %all_to_all.33, f32[]{:T(128)} %broadcast.87), dimensions={1}, to_apply=%all_to_all.24.reduce_sub_computation | reduce | bytes 8388612 | tf_op jit(solution)/shard_map/all_to_all | solution.py:18
  101.0 9.7 %reshape.53 = f32[8192,2,64]{2,1,0:T(2,128)} reshape(f32[16,65536]{1,0:T(8,128)} %reduce.8) | data formatting | bytes 8388608
  110.7 12.2 %copy.26 = f32[2,64,16,512]{3,1,2,0:T(8,128)} copy(f32[2,64,16,512]{1,0,3,2:T(2,128)} %bitcast.96) | data formatting | bytes 8388608 | tf_op jit(solution)/shard_map/all_to_all | solution.py:18
  122.9 17.6 %convolution_bitcast_fusion = f32[1024,1024]{1,0:T(8,128)} fusion(f32[2,1024,512]{2,1,0:T(8,128)} %bitcast.98), kind=kOutput, calls=%fused_computation.4 | convolution fusion | flops 12884901888 | bytes 8388608 | tf_op jit(solution)/shard_map/crm,csm->rs/dot_general | solution.py:20
  140.6 0.0 all-reduce.3.cloned.1.call-update
  140.6 270.4 %all-reduce.3.cloned.1.call-done = f32[1024,1024]{1,0:T(8,128)} async-done(((f32[1024,1024]{1,0:T(8,128)}), f32[1024,1024]{1,0:T(8,128)}) %all-reduce.3.cloned.1.call-update) | async-done | bytes 4194320 | tf_op jit(solution)/shard_map/psum | solution.py:21
  411.0 0.0 copy-done
  411.0 5.5 fusion.32
  416.5 1.8 fusion.33
  418.3 0.1 copy.16
  418.5 11.7 %cholesky.130 = f32[128,128]{1,0:T(8,128)S(1)} custom-call(f32[128,128]{1,0:T(8,128)S(1)} %cholesky.194), custom_call_target="Cholesky" | custom-call | tf_op jit(solution)/shard_map/jit(cholesky)/cholesky | solution.py:11
  430.3 9.8 %custom-call.13 = f32[1,128,128]{1,2,0:T(8,128)S(1)} custom-call(f32[1,128,128]{2,1,0:T(8,128)S(1)} %get-tuple-element.53), custom_call_target="InvertDiagBlocksLowerTriangular" | custom-call | tf_op jit(solution)/shard_map/jit(cholesky)/cholesky | solution.py:11
  440.1 0.2 constant_dynamic-update-slice_fusion.3
  440.3 0.3 convolution_subtract_fusion.3
  440.6 11.7 %cholesky.147 = f32[128,128]{1,0:T(8,128)S(1)} custom-call(f32[128,128]{1,0:T(8,128)S(1)} %convolution_subtract_fusion.3), custom_call_target="Cholesky" | custom-call | tf_op jit(solution)/shard_map/jit(cholesky)/cholesky | solution.py:11
  452.3 0.7 compare_reduce_fusion.2
  467.1 0.1 triangular_solve.75
  467.2 3.9 while.4
  467.2 0.6 fusion.55
  467.8 1.4 bitcast_dynamic-update-slice_fusion.4
  469.2 0.6 fusion.55
  469.8 1.4 bitcast_dynamic-update-slice_fusion.4
  471.2 19.7 %custom-call.14 = f32[2,128,128]{1,2,0:T(8,128)S(1)} custom-call(f32[2,128,128]{2,1,0:T(8,128)S(1)} %get-tuple-element.18), custom_call_target="InvertDiagBlocksLowerTriangular" | custom-call | tf_op jit(solution)/shard_map/jit(_solve_triangular)/triangular_solve | solution.py:12
  490.9 0.6 fusion.8
  491.5 1.0 convolution_subtract_fusion.1
  492.5 0.6 fusion.19
  493.2 5.3 fusion.2
  498.5 1.8 fusion.34
  500.3 0.1 copy.18
  500.5 11.7 %cholesky.164 = f32[128,128]{1,0:T(8,128)S(1)} custom-call(f32[128,128]{1,0:T(8,128)S(1)} %cholesky.197), custom_call_target="Cholesky" | custom-call | tf_op jit(solution)/shard_map/jit(cholesky)/cholesky | solution.py:11
  512.3 9.8 %custom-call.15 = f32[1,128,128]{1,2,0:T(8,128)S(1)} custom-call(f32[1,128,128]{2,1,0:T(8,128)S(1)} %get-tuple-element.49), custom_call_target="InvertDiagBlocksLowerTriangular" | custom-call | tf_op jit(solution)/shard_map/jit(cholesky)/cholesky | solution.py:11
  522.1 0.2 constant_dynamic-update-slice_fusion.1
  522.3 0.3 convolution_subtract_fusion.2
  522.6 11.7 %cholesky.181 = f32[128,128]{1,0:T(8,128)S(1)} custom-call(f32[128,128]{1,0:T(8,128)S(1)} %convolution_subtract_fusion.2), custom_call_target="Cholesky" | custom-call | tf_op jit(solution)/shard_map/jit(cholesky)/cholesky | solution.py:11
  534.3 0.6 compare_reduce_fusion
  535.0 0.6 compare_reduce_fusion.1
  536.9 0.2 select_select_fusion
  537.2 4.0 while.5
  537.2 0.6 fusion.56
  537.8 1.4 bitcast_dynamic-update-slice_fusion.5
  539.2 0.6 fusion.56
  539.8 1.4 bitcast_dynamic-update-slice_fusion.5
  541.2 19.7 %custom-call.16 = f32[2,128,128]{1,2,0:T(8,128)S(1)} custom-call(f32[2,128,128]{2,1,0:T(8,128)S(1)} %get-tuple-element.19), custom_call_target="InvertDiagBlocksLowerTriangular" | custom-call | tf_op jit(solution)/shard_map/jit(_solve_triangular)/triangular_solve | solution.py:12
  560.9 0.6 fusion.6
  561.5 1.0 convolution_subtract_fusion
  562.5 0.6 fusion.15
  563.2 5.7 convolution_bitcast_fusion.1
  568.9 1.8 copy.20
  570.7 4.6 all-to-all-start.1
  575.3 0.1 fusion.13
  575.4 0.7 copy.22
  576.1 17.8 %all-to-all-done.1 = f32[2,256,512]{2,0,1:T(2,128)} async-done(((f32[2,256,512]{2,0,1:T(2,128)}), f32[2,256,512]{2,0,1:T(2,128)}, u32[]{:S(2)}, u32[]{:S(2)}) %all-to-all-start.1) | async-done | bytes 1048608 | tf_op jit(solution)/shard_map/all_to_all | solution.py:26
  593.9 1.8 copy.21
  595.7 1.0 reshape.27
  (18 shorter events, 0.4 us)
Async XLA Ops:
  7.2 403.9 %copy-start = (f32[1024,256]{1,0:T(8,128)S(1)}, f32[1024,256]{1,0:T(8,128)}, u32[]{:S(2)}) copy-start(f32[1024,256]{1,0:T(8,128)} %param.6) | copy-start | bytes 3145732
  7.2 403.8 %all-reduce.3.cloned.1.call-start = ((), (), s32[]{:S(2)}) async-start(), calls=%async_computation.2 | async-start | bytes 8388608 | tf_op jit(solution)/shard_map/psum | solution.py:21
  570.7 23.2 %all-to-all-start.1 = ((f32[2,256,512]{2,0,1:T(2,128)}), f32[2,256,512]{2,0,1:T(2,128)}, u32[]{:S(2)}, u32[]{:S(2)}) async-start(f32[2,256,512]{2,0,1:T(2,128)} %copy.20), calls=%async_computation.1 | async-start | bytes 2097152 | tf_op jit(solution)/shard_map/all_to_all | solution.py:26
Sparse Core Ops, SparseCore 0:
  140.7 270.2 all-reduce.2
where the time goes:
time: 614 us; the launch traced here: 604 us
  waiting for transfers between devices  288 us (47%)
  other arithmetic  122 us (20%)
  local copies, waits for them, and re-layouts  59.5 us (10%)
  blocking collectives  56.1 us (9%)
  matrix products  43.3 us (7%)
  between operations  30.1 us (5%)
    psum x1, waiting for transfers between devices, per_device(): gram = lax.psum(local_gram, ('gx', 'gy', 'gz'))  270 us
    another operation x13, other arithmetic, orthonormal(): lower = jnp.linalg.cholesky(small)  68.5 us
    all_to_all x1, blocking collectives, per_device(): lax.all_to_all(flat_field, 'gx', split_axis=2, concat_axis=1, tiled=True)  56.1 us
    another operation x5, other arithmetic, orthonormal(): return jax.scipy.linalg.solve_triangular(lower, image.T, lower=True).T  39.6 us
    unnamed x6, local copies, waits for them, and re-layouts  33.9 us
    all_to_all x1, waiting for transfers between devices, per_device(): lax.all_to_all(projected, 'gx', split_axis=1, concat_axis=2, tiled=True)  17.8 us
    dot_general x1, matrix products, per_device(): jnp.einsum('crm,csm->rs', fibers, fibers, precision=lax.Precision.HIGHEST)  17.6 us
    all_to_all x1, other arithmetic, per_device(): lax.all_to_all(flat_field, 'gx', split_axis=2, concat_axis=1, tiled=True)  13.7 us
  transfers between devices with their start and end apart: 2, of which 2 were waited for; matrix products, arithmetic and copies ran while one was open for 0% of the time, Pallas kernels for 0%

commit v1 on v0

--- a/solution.py
+++ b/solution.py
@@ -18,7 +18,7 @@
     fibers = lax.all_to_all(flat_field, "gx", split_axis=2, concat_axis=1, tiled=True)
     basis = start_basis
     local_gram = jnp.einsum("crm,csm->rs", fibers, fibers, precision=lax.Precision.HIGHEST)
-    gram = lax.psum(local_gram, ("gx", "gy", "gz"))
+    gram = lax.psum(lax.psum(local_gram, "gx"), ("gy", "gz"))
     for step in range(ITERS):
         image = jnp.dot(gram, basis, precision=lax.Precision.HIGHEST)
         basis = orthonormal(image)

time: 614 us -> 584 us (0.951)
  waiting for transfers between devices: 288 us -> 256 us
    psum x1 -> x2, waiting for transfers between devices: 270 us -> 238 us  [per_device(): gram = lax.psum(lax.psum(local_gram, 'gx'), ('gy', 'gz'))]
  transfers between devices with their start and end apart: 2 -> 3, of which waited for: 2 -> 3; matrix products, arithmetic and copies ran while one was open for 0% -> 0% of each run, Pallas kernels for 0% -> 0%
where the time goes in v1:
time: 584 us; the launch traced here: 574 us
  waiting for transfers between devices  256 us (44%)
  other arithmetic  122 us (21%)
  local copies, waits for them, and re-layouts  59.5 us (10%)
  blocking collectives  56.1 us (10%)
  matrix products  43.1 us (7%)
  between operations  30.1 us (5%)
  starting transfers between devices  6.9 us (1%)
    psum x2, waiting for transfers between devices, per_device(): gram = lax.psum(lax.psum(local_gram, 'gx'), ('gy', 'gz'))  238 us
    another operation x13, other arithmetic, orthonormal(): lower = jnp.linalg.cholesky(small)  68.5 us
    all_to_all x1, blocking collectives, per_device(): lax.all_to_all(flat_field, 'gx', split_axis=2, concat_axis=1, tiled=True)  56.1 us
    another operation x5, other arithmetic, orthonormal(): return jax.scipy.linalg.solve_triangular(lower, image.T, lower=True).T  39.6 us
    unnamed x6, local copies, waits for them, and re-layouts  33.9 us
    all_to_all x1, waiting for transfers between devices, per_device(): lax.all_to_all(projected, 'gx', split_axis=1, concat_axis=2, tiled=True)  17.8 us
    dot_general x1, matrix products, per_device(): jnp.einsum('crm,csm->rs', fibers, fibers, precision=lax.Precision.HIGHEST)  17.6 us
    all_to_all x1, other arithmetic, per_device(): lax.all_to_all(flat_field, 'gx', split_axis=2, concat_axis=1, tiled=True)  13.7 us
  transfers between devices with their start and end apart: 3, of which 3 were waited for; matrix products, arithmetic and copies ran while one was open for 0% of the time, Pallas kernels for 0%

profile of v1, /device:TPU:97, one launch (start us, length us, event | category | flops | bytes accessed | tf_op | source)
XLA Modules:
  0.0 573.8 jit_solution(17223868047990297946)
XLA Ops:
  7.2 0.0 copy-start
  7.2 0.0 all-reduce.4.cloned.1.call-start
  7.2 8.4 %copy.13 = f32[2,64,64,128]{1,0,3,2:T(2,128)} copy(f32[2,64,64,128]{3,2,1,0:T(8,128)} %param.5) | data formatting | bytes 8388608 | tf_op args[0]
  15.7 15.1 %reshape.52 = f32[16,1,65536]{2,1,0:T(1,128)} reshape(f32[8192,2,64]{2,1,0:T(2,128)} %bitcast.97) | data formatting | bytes 8388608
  30.8 56.1 %all_to_all.33 = f32[16,1,65536]{2,1,0:T(1,128)} all-to-all(f32[16,1,65536]{2,1,0:T(1,128)} %reshape.52), channel_id=1, replica_groups=mesh['gx'=16,'gy'=2,'gz'=8] {'gx'}, dimensions={0} | all-to-all | bytes 8388608 | tf_op jit(solution)/shard_map/all_to_all | solution.py:18
  86.8 0.5 broadcast.87
  87.3 13.7 %reduce.8 = f32[16,65536]{1,0:T(8,128)} reduce(f32[16,1,65536]{2,1,0:T(1,128)} %all_to_all.33, f32[]{:T(128)} %broadcast.87), dimensions={1}, to_apply=%all_to_all.24.reduce_sub_computation | reduce | bytes 8388612 | tf_op jit(solution)/shard_map/all_to_all | solution.py:18
  101.0 9.7 %reshape.53 = f32[8192,2,64]{2,1,0:T(2,128)} reshape(f32[16,65536]{1,0:T(8,128)} %reduce.8) | data formatting | bytes 8388608
  110.7 12.2 %copy.26 = f32[2,64,16,512]{3,1,2,0:T(8,128)} copy(f32[2,64,16,512]{1,0,3,2:T(2,128)} %bitcast.96) | data formatting | bytes 8388608 | tf_op jit(solution)/shard_map/all_to_all | solution.py:18
  122.9 17.6 %convolution_bitcast_fusion = f32[1024,1024]{1,0:T(8,128)} fusion(f32[2,1024,512]{2,1,0:T(8,128)} %bitcast.98), kind=kOutput, calls=%fused_computation.4 | convolution fusion | flops 12884901888 | bytes 8388608 | tf_op jit(solution)/shard_map/crm,csm->rs/dot_general | solution.py:20
  140.6 0.0 all-reduce.4.cloned.1.call-update
  140.6 0.3 all-reduce.6.cloned.1.call-start
  140.9 114.2 %all-reduce.4.cloned.1.call-done = f32[1024,1024]{1,0:T(8,128)} async-done(((f32[1024,1024]{1,0:T(8,128)}), f32[1024,1024]{1,0:T(8,128)}) %all-reduce.4.cloned.1.call-update) | async-done | bytes 4194320 | tf_op jit(solution)/shard_map/psum | solution.py:21
  255.0 0.0 all-reduce.6.cloned.1.call-update
  255.1 124.0 %all-reduce.6.cloned.1.call-done = f32[1024,1024]{1,0:T(8,128)} async-done(((f32[1024,1024]{1,0:T(8,128)}), f32[1024,1024]{1,0:T(8,128)}) %all-reduce.6.cloned.1.call-update) | async-done | bytes 4194320 | tf_op jit(solution)/shard_map/psum | solution.py:21
  379.0 0.0 copy-done
  379.0 5.2 fusion.32
  384.3 1.8 fusion.33
  386.1 0.1 copy.16
  386.3 11.7 %cholesky.130 = f32[128,128]{1,0:T(8,128)S(1)} custom-call(f32[128,128]{1,0:T(8,128)S(1)} %cholesky.194), custom_call_target="Cholesky" | custom-call | tf_op jit(solution)/shard_map/jit(cholesky)/cholesky | solution.py:11
  398.1 9.8 %custom-call.13 = f32[1,128,128]{1,2,0:T(8,128)S(1)} custom-call(f32[1,128,128]{2,1,0:T(8,128)S(1)} %get-tuple-element.53), custom_call_target="InvertDiagBlocksLowerTriangular" | custom-call | tf_op jit(solution)/shard_map/jit(cholesky)/cholesky | solution.py:11
  407.9 0.2 constant_dynamic-update-slice_fusion.3
  408.1 0.3 convolution_subtract_fusion.3
  408.4 11.7 %cholesky.147 = f32[128,128]{1,0:T(8,128)S(1)} custom-call(f32[128,128]{1,0:T(8,128)S(1)} %convolution_subtract_fusion.3), custom_call_target="Cholesky" | custom-call | tf_op jit(solution)/shard_map/jit(cholesky)/cholesky | solution.py:11
  420.1 0.7 compare_reduce_fusion.2
  434.9 0.1 triangular_solve.75
  435.0 3.9 while.4
  435.1 0.6 fusion.55
  435.6 1.4 bitcast_dynamic-update-slice_fusion.4
  437.0 0.6 fusion.55
  437.6 1.4 bitcast_dynamic-update-slice_fusion.4
  439.0 19.7 %custom-call.14 = f32[2,128,128]{1,2,0:T(8,128)S(1)} custom-call(f32[2,128,128]{2,1,0:T(8,128)S(1)} %get-tuple-element.18), custom_call_target="InvertDiagBlocksLowerTriangular" | custom-call | tf_op jit(solution)/shard_map/jit(_solve_triangular)/triangular_solve | solution.py:12
  458.7 0.6 fusion.8
  459.3 1.0 convolution_subtract_fusion.1
  460.3 0.6 fusion.19
  461.0 5.3 fusion.2
  466.3 1.8 fusion.34
  468.1 0.1 copy.18
  468.3 11.7 %cholesky.164 = f32[128,128]{1,0:T(8,128)S(1)} custom-call(f32[128,128]{1,0:T(8,128)S(1)} %cholesky.197), custom_call_target="Cholesky" | custom-call | tf_op jit(solution)/shard_map/jit(cholesky)/cholesky | solution.py:11
  480.1 9.8 %custom-call.15 = f32[1,128,128]{1,2,0:T(8,128)S(1)} custom-call(f32[1,128,128]{2,1,0:T(8,128)S(1)} %get-tuple-element.49), custom_call_target="InvertDiagBlocksLowerTriangular" | custom-call | tf_op jit(solution)/shard_map/jit(cholesky)/cholesky | solution.py:11
  489.9 0.2 constant_dynamic-update-slice_fusion.1
  490.1 0.3 convolution_subtract_fusion.2
  490.4 11.7 %cholesky.181 = f32[128,128]{1,0:T(8,128)S(1)} custom-call(f32[128,128]{1,0:T(8,128)S(1)} %convolution_subtract_fusion.2), custom_call_target="Cholesky" | custom-call | tf_op jit(solution)/shard_map/jit(cholesky)/cholesky | solution.py:11
  502.2 0.6 compare_reduce_fusion
  502.8 0.6 compare_reduce_fusion.1
  504.7 0.2 select_select_fusion
  505.0 4.0 while.5
  505.0 0.6 fusion.56
  505.6 1.4 bitcast_dynamic-update-slice_fusion.5
  507.0 0.6 fusion.56
  507.6 1.4 bitcast_dynamic-update-slice_fusion.5
  509.0 19.7 %custom-call.16 = f32[2,128,128]{1,2,0:T(8,128)S(1)} custom-call(f32[2,128,128]{2,1,0:T(8,128)S(1)} %get-tuple-element.19), custom_call_target="InvertDiagBlocksLowerTriangular" | custom-call | tf_op jit(solution)/shard_map/jit(_solve_triangular)/triangular_solve | solution.py:12
  528.7 0.6 fusion.6
  529.3 1.0 convolution_subtract_fusion
  530.3 0.6 fusion.15
  531.0 5.7 convolution_bitcast_fusion.1
  536.7 1.8 copy.20
  538.5 6.6 %all-to-all-start.1 = ((f32[2,256,512]{2,0,1:T(2,128)}), f32[2,256,512]{2,0,1:T(2,128)}, u32[]{:S(2)}, u32[]{:S(2)}) async-start(f32[2,256,512]{2,0,1:T(2,128)} %copy.20), calls=%async_computation.1 | async-start | bytes 2097152 | tf_op jit(solution)/shard_map/all_to_all | solution.py:26
  545.1 0.1 fusion.13
  545.2 0.7 copy.22
  545.9 17.8 %all-to-all-done.1 = f32[2,256,512]{2,0,1:T(2,128)} async-done(((f32[2,256,512]{2,0,1:T(2,128)}), f32[2,256,512]{2,0,1:T(2,128)}, u32[]{:S(2)}, u32[]{:S(2)}) %all-to-all-start.1) | async-done | bytes 1048608 | tf_op jit(solution)/shard_map/all_to_all | solution.py:26
  563.7 1.8 copy.21
  565.5 1.0 reshape.27
  (18 shorter events, 0.4 us)
Async XLA Ops:
  7.2 371.9 %copy-start = (f32[1024,256]{1,0:T(8,128)S(1)}, f32[1024,256]{1,0:T(8,128)}, u32[]{:S(2)}) copy-start(f32[1024,256]{1,0:T(8,128)} %param.6) | copy-start | bytes 3145732
  7.2 247.9 %all-reduce.4.cloned.1.call-start = ((), (), s32[]{:S(2)}) async-start(), calls=%async_computation.2 | async-start | bytes 8388608 | tf_op jit(solution)/shard_map/psum | solution.py:21
  140.6 238.5 %all-reduce.6.cloned.1.call-start = ((), (), s32[]{:S(2)}) async-start(), calls=%async_computation.3 | async-start | bytes 8388608 | tf_op jit(solution)/shard_map/psum | solution.py:21
  538.5 25.2 %all-to-all-start.1 = ((f32[2,256,512]{2,0,1:T(2,128)}), f32[2,256,512]{2,0,1:T(2,128)}, u32[]{:S(2)}, u32[]{:S(2)}) async-start(f32[2,256,512]{2,0,1:T(2,128)} %copy.20), calls=%async_computation.1 | async-start | bytes 2097152 | tf_op jit(solution)/shard_map/all_to_all | solution.py:26
Sparse Core Ops, SparseCore 0:
  140.7 114.2 all-reduce.3
  257.4 121.5 all-reduce.5
